TPU v7x, 32 devices: a whole 2x2x4 slice. The times are simulated.
32 devices in a mesh: bin: 4 (over x, core), fsdp: 8 (over z, y).
Axes of the slice: x: 2, y: 2, z: 4, core: 2. Of those that a mesh axis runs over, the one named last changes fastest.
Arguments:
- latents: bfloat16 [4, 16, 256, 1152], P('bin', 'fsdp'), may hold values from -6 to 6
- cond: float32 [4, 1152], P('bin'), may hold values from -6 to 6
- live: int32 [4, 8], P('bin', 'fsdp'), may hold values from 1 to 2, 12 in all within a row
- w_ada: bfloat16 [1152, 6912], P(None, 'fsdp'), may hold values from -0.375 to 0.375
- b_ada: bfloat16 [6912], P('fsdp'), may hold values from -3 to 3
- w_qkv: bfloat16 [1152, 3456], P('fsdp'), may hold values from -0.1875 to 0.1875
- b_qv: bfloat16 [2304], P('fsdp'), may hold values from -3 to 3
- w_proj: bfloat16 [1152, 1152], P('fsdp'), may hold values from -0.5 to 0.5
- b_proj: bfloat16 [1152], P('fsdp'), may hold values from -3 to 3
- w_fc1: bfloat16 [1152, 4608], P('fsdp'), may hold values from -0.1875 to 0.1875
- b_fc1: bfloat16 [4608], P('fsdp'), may hold values from -3 to 3
- w_fc2: bfloat16 [4608, 1152], P('fsdp'), may hold values from -0.09375 to 0.09375
- b_fc2: bfloat16 [1152], P('fsdp'), may hold values from -3 to 3
- cotangent: bfloat16 [4, 16, 256, 1152], P('bin', 'fsdp'), may hold values from -6 to 6
Outputs:
- block_out: bfloat16 [4, 16, 256, 1152], P('bin', 'fsdp')
- latents_grad: float32 [4, 16, 256, 1152], P('bin', 'fsdp')
- cond_grad: float32 [4, 1152], P('bin')
- w_ada_grad: float32 [1152, 6912], P(None, 'fsdp')
- b_ada_grad: float32 [6912], P('fsdp')
- w_qkv_grad: float32 [1152, 3456], P('fsdp')
- b_qv_grad: float32 [2304], P('fsdp')
- w_proj_grad: float32 [1152, 1152], P('fsdp')
- b_proj_grad: float32 [1152], P('fsdp')
- w_fc1_grad: float32 [1152, 4608], P('fsdp')
- b_fc1_grad: float32 [4608], P('fsdp')
- w_fc2_grad: float32 [4608, 1152], P('fsdp')
- b_fc2_grad: float32 [1152], P('fsdp')
Inputs may be any that keep to these rules, and one draw needn't show every extreme that they name: The counts of one bin's devices sum to 12; every bin has a device with 2 live images; a device's live images are its first slots.
All inputs are finite; a program needn't handle non-finite values.
Results may differ from a plain program's by a relative error of at most 0.015.
The roundings to bfloat16 on the way count: a program that leaves them out, or rounds other values in their place, can miss the bound.
Values may be sent and summed in bfloat16 or wider, within the bound.
A program may use at most 256 MiB of HBM per device.

v0:
```python
import jax
import jax.numpy as jnp
from jax import lax
from jax.sharding import PartitionSpec as P

HEAD_DIM = 72


def layer_norm(field):
    center = field - jnp.mean(field, axis=-1, keepdims=True)
    return center * lax.rsqrt(jnp.mean(center * center, axis=-1, keepdims=True) + 1e-06)


def gelu_tanh(field):
    return (
        0.5
        * field
        * (1.0 + jnp.tanh(0.7978845608028654 * (field + 0.044715 * field * field * field)))
    )


def modulate(field, shift_vec, scale_vec):
    return layer_norm(field) * (1.0 + scale_vec) + shift_vec


def pair_scores(query_block, key_block):
    return jnp.einsum(
        "gqhd,gkhd->ghqk", query_block, key_block, preferred_element_type=jnp.float32
    ) * HEAD_DIM ** (-0.5)


def attend_pair(group_item):
    query_block, key_block, value_block = group_item
    scores = pair_scores(query_block, key_block)
    highest = jnp.max(scores, axis=-1, keepdims=True)
    exp_scores = jnp.exp(scores - highest)
    totals = jnp.sum(exp_scores, axis=-1, keepdims=True)
    attn_probs = (exp_scores / totals).astype(jnp.bfloat16)
    attended = jnp.einsum(
        "ghqk,gkhd->gqhd", attn_probs, value_block, preferred_element_type=jnp.float32
    )
    return (attended, (highest + jnp.log(totals))[..., 0])


def attend_back(group_item):
    query_block, key_block, value_block, log_total, grad_att = group_item
    scores = pair_scores(query_block, key_block)
    attn_probs = jnp.exp(scores - log_total[..., None])
    grad_probs = jnp.einsum(
        "gqhd,gkhd->ghqk", grad_att, value_block, preferred_element_type=jnp.float32
    )
    row_terms = jnp.sum(attn_probs * grad_probs, axis=-1, keepdims=True)
    grad_scores = (attn_probs * (grad_probs - row_terms)).astype(jnp.bfloat16)
    grad_query = jnp.einsum(
        "ghqk,gkhd->gqhd", grad_scores, key_block, preferred_element_type=jnp.float32
    ) * HEAD_DIM ** (-0.5)
    grad_key = jnp.einsum(
        "ghqk,gqhd->gkhd", grad_scores, query_block, preferred_element_type=jnp.float32
    ) * HEAD_DIM ** (-0.5)
    grad_value = jnp.einsum(
        "ghqk,gqhd->gkhd",
        attn_probs.astype(jnp.bfloat16),
        grad_att,
        preferred_element_type=jnp.float32,
    )
    return jnp.stack([grad_query, grad_key, grad_value], axis=2)


def run_block(flat_rows, modulation, weights, images, length):
    full_qkv, full_proj, full_fc1, full_fc2, bias_qv, bias_proj, bias_fc1, bias_fc2 = weights
    width = flat_rows.shape[1]
    heads = width // HEAD_DIM
    pieces = jnp.split(modulation, 6)
    h_first = modulate(flat_rows, pieces[0], pieces[1]).astype(jnp.bfloat16)
    qkv_bias = jnp.concatenate(
        [bias_qv[:width], jnp.zeros((width,), jnp.bfloat16), bias_qv[width:]]
    ).astype(jnp.float32)
    qkv_rows = (jnp.dot(h_first, full_qkv, preferred_element_type=jnp.float32) + qkv_bias).astype(
        jnp.bfloat16
    )
    split_rows = qkv_rows.reshape(images // 2, 2, length, 3, heads, HEAD_DIM)
    attended, log_total = lax.map(
        attend_pair, (split_rows[:, :, :, 0], split_rows[:, :, :, 1], split_rows[:, :, :, 2])
    )
    attended = attended.reshape(images * length, width).astype(jnp.bfloat16)
    branch = jnp.dot(attended, full_proj, preferred_element_type=jnp.float32) + bias_proj.astype(
        jnp.float32
    )
    middle = flat_rows + pieces[2] * branch
    h_second = modulate(middle, pieces[3], pieces[4]).astype(jnp.bfloat16)
    pre_act = jnp.dot(h_second, full_fc1, preferred_element_type=jnp.float32) + bias_fc1.astype(
        jnp.float32
    )
    hidden = gelu_tanh(pre_act).astype(jnp.bfloat16)
    mlp_out = jnp.dot(hidden, full_fc2, preferred_element_type=jnp.float32) + bias_fc2.astype(
        jnp.float32
    )
    result = middle + pieces[5] * mlp_out
    return (
        h_first,
        split_rows,
        log_total,
        attended,
        branch,
        middle,
        h_second,
        pre_act,
        hidden,
        mlp_out,
        result,
    )


def on_device(
    latents,
    cond,
    live,
    w_ada,
    b_ada,
    w_qkv,
    b_qv,
    w_proj,
    b_proj,
    w_fc1,
    b_fc1,
    w_fc2,
    b_fc2,
    cotangent,
):
    images = latents.shape[1]
    length = latents.shape[2]
    width = latents.shape[3]
    heads = width // HEAD_DIM
    scaled = jax.nn.silu(cond[0]).astype(jnp.bfloat16)
    mod_part = jnp.dot(scaled, w_ada, preferred_element_type=jnp.float32) + b_ada.astype(
        jnp.float32
    )
    modulation = lax.all_gather(mod_part, "fsdp", axis=0, tiled=True)
    gathered = (
        lax.all_gather(w_qkv, "fsdp", axis=0, tiled=True),
        lax.all_gather(w_proj, "fsdp", axis=0, tiled=True),
        lax.all_gather(w_fc1, "fsdp", axis=0, tiled=True),
        lax.all_gather(w_fc2, "fsdp", axis=0, tiled=True),
        lax.all_gather(b_qv, "fsdp", axis=0, tiled=True),
        lax.all_gather(b_proj, "fsdp", axis=0, tiled=True),
        lax.all_gather(b_fc1, "fsdp", axis=0, tiled=True),
        lax.all_gather(b_fc2, "fsdp", axis=0, tiled=True),
    )
    flat_rows = latents[0].reshape(images * length, width).astype(jnp.float32)
    live_mask = (lax.iota(jnp.int32, images) < live[0, 0]).astype(jnp.float32)
    row_mask = jnp.repeat(live_mask, length)[:, None]
    forward_run = run_block(flat_rows, modulation, gathered, images, length)
    block_out = (forward_run[10] * row_mask).astype(jnp.bfloat16).reshape(latents.shape)
    weights = (
        lax.all_gather(w_qkv, "fsdp", axis=0, tiled=True),
        lax.all_gather(w_proj, "fsdp", axis=0, tiled=True),
        lax.all_gather(w_fc1, "fsdp", axis=0, tiled=True),
        lax.all_gather(w_fc2, "fsdp", axis=0, tiled=True),
        lax.all_gather(b_qv, "fsdp", axis=0, tiled=True),
        lax.all_gather(b_proj, "fsdp", axis=0, tiled=True),
        lax.all_gather(b_fc1, "fsdp", axis=0, tiled=True),
        lax.all_gather(b_fc2, "fsdp", axis=0, tiled=True),
    )
    full_qkv, full_proj, full_fc1, full_fc2 = (weights[0], weights[1], weights[2], weights[3])
    saved = run_block(flat_rows, modulation, weights, images, length)
    (
        h_first,
        split_rows,
        log_total,
        attended,
        branch,
        middle,
        h_second,
        pre_act,
        hidden,
        mlp_out,
        result,
    ) = saved
    pieces = jnp.split(modulation, 6)
    grad_res = cotangent[0].reshape(images * length, width).astype(jnp.float32) * row_mask
    grad_out = (pieces[5] * grad_res).astype(jnp.bfloat16)
    grad_gate_two = jnp.sum(grad_res * mlp_out, axis=0)
    grad_fc2 = jnp.einsum("rf,rd->fd", hidden, grad_out, preferred_element_type=jnp.float32)
    grad_bfc2 = jnp.sum(grad_out.astype(jnp.float32), axis=0)
    grad_hidden = jnp.einsum("rd,fd->rf", grad_out, full_fc2, preferred_element_type=jnp.float32)
    gelu_pull = jax.vjp(gelu_tanh, pre_act)[1]
    grad_pre = gelu_pull(grad_hidden)[0].astype(jnp.bfloat16)
    grad_fc1 = jnp.einsum("rd,rf->df", h_second, grad_pre, preferred_element_type=jnp.float32)
    grad_bfc1 = jnp.sum(grad_pre.astype(jnp.float32), axis=0)
    grad_h2 = jnp.einsum("rf,df->rd", grad_pre, full_fc1, preferred_element_type=jnp.float32)
    second_pull = jax.vjp(modulate, middle, pieces[3], pieces[4])[1]
    grad_mid_norm, grad_shift_two, grad_scale_two = second_pull(grad_h2)
    grad_mid = grad_res + grad_mid_norm
    grad_branch = (pieces[2] * grad_mid).astype(jnp.bfloat16)
    grad_gate_one = jnp.sum(grad_mid * branch, axis=0)
    grad_proj = jnp.einsum("rd,re->de", attended, grad_branch, preferred_element_type=jnp.float32)
    grad_bproj = jnp.sum(grad_branch.astype(jnp.float32), axis=0)
    grad_att = jnp.einsum(
        "re,de->rd", grad_branch, full_proj, preferred_element_type=jnp.float32
    ).astype(jnp.bfloat16)
    grad_att = grad_att.reshape(images // 2, 2, length, heads, HEAD_DIM)
    grad_qkv = lax.map(
        attend_back,
        (
            split_rows[:, :, :, 0],
            split_rows[:, :, :, 1],
            split_rows[:, :, :, 2],
            log_total,
            grad_att,
        ),
    )
    grad_qkv = grad_qkv.reshape(images * length, 3 * width).astype(jnp.bfloat16)
    grad_wqkv = jnp.einsum("rd,re->de", h_first, grad_qkv, preferred_element_type=jnp.float32)
    qkv_sums = jnp.sum(grad_qkv.astype(jnp.float32), axis=0)
    grad_bqv = jnp.concatenate([qkv_sums[:width], qkv_sums[2 * width :]])
    grad_h1 = jnp.einsum("re,de->rd", grad_qkv, full_qkv, preferred_element_type=jnp.float32)
    first_pull = jax.vjp(modulate, flat_rows, pieces[0], pieces[1])[1]
    grad_rows_norm, grad_shift_one, grad_scale_one = first_pull(grad_h1)
    grad_rows = grad_mid + grad_rows_norm
    grad_mod = jnp.concatenate(
        [
            grad_shift_one,
            grad_scale_one,
            grad_gate_one,
            grad_shift_two,
            grad_scale_two,
            grad_gate_two,
        ]
    )
    shards = (
        lax.psum_scatter(grad_wqkv, "fsdp", scatter_dimension=0, tiled=True),
        lax.psum_scatter(grad_proj, "fsdp", scatter_dimension=0, tiled=True),
        lax.psum_scatter(grad_fc1, "fsdp", scatter_dimension=0, tiled=True),
        lax.psum_scatter(grad_fc2, "fsdp", scatter_dimension=0, tiled=True),
        lax.psum_scatter(grad_bqv, "fsdp", scatter_dimension=0, tiled=True),
        lax.psum_scatter(grad_bproj, "fsdp", scatter_dimension=0, tiled=True),
        lax.psum_scatter(grad_bfc1, "fsdp", scatter_dimension=0, tiled=True),
        lax.psum_scatter(grad_bfc2, "fsdp", scatter_dimension=0, tiled=True),
        lax.psum_scatter(grad_mod, "fsdp", scatter_dimension=0, tiled=True),
    )
    mod_mine = shards[8]
    grad_wada = scaled.astype(jnp.float32)[:, None] * mod_mine[None, :]
    grad_scaled = jnp.dot(w_ada.astype(jnp.float32), mod_mine, precision=lax.Precision.HIGHEST)
    grad_scaled = lax.psum(grad_scaled, "fsdp")
    silu_pull = jax.vjp(jax.nn.silu, cond[0])[1]
    grad_cond = silu_pull(grad_scaled)[0][None, :]
    totals = lax.psum(
        (
            shards[0],
            shards[1],
            shards[2],
            shards[3],
            shards[4],
            shards[5],
            shards[6],
            shards[7],
            grad_wada,
            mod_mine,
        ),
        "bin",
    )
    return (
        block_out,
        grad_rows.reshape(latents.shape),
        grad_cond,
        totals[8],
        totals[9],
        totals[0],
        totals[4],
        totals[1],
        totals[5],
        totals[2],
        totals[6],
        totals[3],
        totals[7],
    )


def solution(mesh):
    return jax.shard_map(
        on_device,
        mesh=mesh,
        in_specs=(
            P("bin", "fsdp", None, None),
            P("bin", None),
            P("bin", "fsdp"),
            P(None, "fsdp"),
            P("fsdp"),
            P("fsdp", None),
            P("fsdp"),
            P("fsdp", None),
            P("fsdp"),
            P("fsdp", None),
            P("fsdp"),
            P("fsdp", None),
            P("fsdp"),
            P("bin", "fsdp", None, None),
        ),
        out_specs=(
            P("bin", "fsdp", None, None),
            P("bin", "fsdp", None, None),
            P("bin", None),
            P(None, "fsdp"),
            P("fsdp"),
            P("fsdp", None),
            P("fsdp"),
            P("fsdp", None),
            P("fsdp"),
            P("fsdp", None),
            P("fsdp"),
            P("fsdp", None),
            P("fsdp"),
        ),
        check_vma=False,
    )
```

profile of v0, /device:TPU:0, one launch (start us, length us, event | category | flops | bytes accessed | tf_op | source)
XLA Modules:
  0.0 1843.6 jit_solution(338678586922015093)
XLA Ops:
  16.1 40.7 %all-reduce.13 = (bf16[2304]{0:T(1024)(128)(2,1)S(1)}, bf16[1152]{0:T(1024)(128)(2,1)S(1)}, bf16[1152]{0:T(1024)(128)(2,1)}, bf16[4608]{0:T(1024)(128)(2,1)S(1)}) all-reduce(bf16[2304]{0:T(1024)(128)(2,1)S(1)} %dynamic-update-slice.1, bf16[1152]{0:T(1024)(128)(2,1)S(1)} %dynamic-update-slice.2, ...), channel_id=1, replica_groups=mesh['bin'=4,'fsdp'=8] {'fsdp'}, use_global_device_ids=true, to_apply=%add.1 | all-reduce | flops 9216 | bytes 36864
  58.9 34.5 %all-reduce = f32[6912]{0:T(1024)S(1)} all-reduce(f32[6912]{0:T(1024)S(1)} %add_dynamic-update-slice_fusion), channel_id=1, replica_groups=mesh['bin'=4,'fsdp'=8] {'fsdp'}, use_global_device_ids=true, to_apply=%add | all-reduce | flops 6912 | bytes 55296
  93.5 2.6 multiply_convert_fusion.4
  96.2 1.5 fusion.21
  97.7 36.3 %all-gather.5.cloned.1.call-done = bf16[1152,3456]{1,0:T(8,128)(2,1)} async-done(((bf16[144,3456]{1,0:T(8,128)(2,1)}), bf16[1152,3456]{1,0:T(8,128)(2,1)}) %all-gather.5.cloned.1.call-update) | async-done | bytes 7962640 | tf_op jit(solution)/shard_map/all_gather | solution.py:140
  134.0 10.3 add_convert_fusion
  144.3 13.6 reshape.274
  157.9 6.0 fusion.57
  163.9 4.1 copy.72
  168.0 4.1 copy.71
  172.2 4.1 copy.70
  176.3 2.9 multiply_reduce_fusion.1
  179.3 1.6 fusion.6
  180.9 1.7 copy-done.1
  182.6 14.0 fusion.32
  199.1 6.0 fusion.56
  205.1 1.4 copy-done.3
  206.9 135.9 %all-gather.9.cloned.1.call-done = bf16[1152,4608]{1,0:T(8,128)(2,1)} async-done(((bf16[144,4608]{1,0:T(8,128)(2,1)}), bf16[1152,4608]{1,0:T(8,128)(2,1)}) %all-gather.9.cloned.1.call-update) | async-done | bytes 10616848 | tf_op jit(solution)/shard_map/all_gather | solution.py:142
  342.8 12.2 fusion.51
  355.0 140.5 %all-gather.11.cloned.1.call-done = bf16[4608,1152]{1,0:T(8,128)(2,1)} async-done(((bf16[576,1152]{1,0:T(8,128)(2,1)}), bf16[4608,1152]{1,0:T(8,128)(2,1)}) %all-gather.11.cloned.1.call-update) | async-done | bytes 10616848 | tf_op jit(solution)/shard_map/all_gather | solution.py:143
  495.5 18.9 %convert_reduce_fusion = (f32[4608]{0:T(1024)S(1)}, bf16[512,4608]{1,0:T(8,128)(2,1)}) fusion(f32[512,4608]{1,0:T(8,128)} %fusion.51, f32[4608]{0:T(1024)S(1)} %convert_element_type.166, bf16[512,1152]{1,0:T(8,128)(2,1)} %multiply_convert_fusion.4, bf16[4608,1152]{1,0:T(8,128)(2,1)} %all-gather.11.cloned.1.call-done), kind=kOutput, calls=%fused_computation.10 | convolution fusion | flops 5499514368 | bytes 25989120 | tf_op jit(solution)/shard_map/rd,fd->rf/dot_general | solution.py:185
  514.3 11.6 multiply_reduce_fusion.3
  529.1 4.0 fusion.63
  533.6 1.6 fusion.26
  535.2 4.7 convolution_convert_fusion
  539.9 5.7 reshape.275
  545.6 4.1 copy.56
  549.7 6.6 multiply_reduce_fusion
  556.4 4.8 multiply_convert_fusion.1
  563.9 1.6 fusion.28
  566.7 3.6 copy.61
  571.2 1.8 copy-done.16
  572.9 7.9 fusion.62
  580.9 13.0 fusion.50
  594.0 14.8 fusion.52
  610.2 9.9 fusion.27
  622.2 15.5 multiply_reduce_fusion.2
  637.8 35.9 %all-reduce.5 = f32[6912]{0:T(1024)S(1)} all-reduce(f32[6912]{0:T(1024)S(1)} %constant_dynamic-update-slice_fusion), channel_id=2, replica_groups=mesh['bin'=4,'fsdp'=8] {'fsdp'}, use_global_device_ids=true, to_apply=%region_17.18.clone | all-reduce | flops 6912 | bytes 55296
  673.8 2.3 broadcast_multiply_fusion
  676.0 232.5 %reduce-scatter.5.cloned.1.call-done = f32[144,3456]{1,0:T(8,128)} async-done(((f32[1152,3456]{1,0:T(8,128)}), f32[144,3456]{1,0:T(8,128)}) %reduce-scatter.5.cloned.1.call-update) | async-done | bytes 1990672 | tf_op jit(solution)/shard_map/reduce_scatter | solution.py:231
  908.6 350.7 %reduce-scatter.9.cloned.1.call-done = f32[144,4608]{1,0:T(8,128)} async-done(((f32[1152,4608]{1,0:T(8,128)}), f32[144,4608]{1,0:T(8,128)}) %reduce-scatter.9.cloned.1.call-update) | async-done | bytes 2654224 | tf_op jit(solution)/shard_map/reduce_scatter | solution.py:233
  1259.3 350.3 %reduce-scatter.11.cloned.1.call-done = f32[576,1152]{1,0:T(8,128)} async-done(((f32[4608,1152]{1,0:T(8,128)}), f32[576,1152]{1,0:T(8,128)}) %reduce-scatter.11.cloned.1.call-update) | async-done | bytes 2654224 | tf_op jit(solution)/shard_map/reduce_scatter | solution.py:234
  1613.2 35.7 %all-reduce.10 = (f32[1152]{0:T(1024)S(1)}, f32[2304]{0:T(1024)S(1)}, f32[1152]{0:T(1024)S(1)}, f32[4608]{0:T(1024)S(1)}, f32[1152]{0:T(1024)S(1)}) all-reduce(f32[1152]{0:T(1024)S(1)} %convolution_reduce_fusion, f32[2304]{0:T(1024)S(1)} %pad_maximum_fusion, ...), channel_id=1, replica_groups=mesh['bin'=4,'fsdp'=8] {'fsdp'}, use_global_device_ids=true, to_apply=%region_18.19 | all-reduce | flops 10368 | bytes 82944 | tf_op jit(solution)/shard_map/psum | solution.py:244
  1649.9 12.5 all-reduce.11
  1662.4 162.9 %all-reduce.16.cloned.1.call-done = (f32[1152,864]{0,1:T(8,128)}, f32[144,3456]{1,0:T(8,128)}, f32[144,1152]{1,0:T(8,128)}, f32[144,4608]{1,0:T(8,128)}, f32[576,1152]{1,0:T(8,128)}) async-done(((f32[1152,864]{0,1:T(8,128)}, f32[144,3456]{1,0:T(8,128)}, f32[144,1152]{1,0:T(8,128)}, f32[144,4608]{1,0:T(8,128)}, f32[576,1152]{1,0:T(8,128)}), (f32[1152,864]{0,1:T(8,128)}, f32[144,3456]{1,0:T(8,128)}, ...) | async-done | bytes 11943952 | tf_op jit(solution)/shard_map/psum | solution.py:247
  1825.2 4.5 copy.95
  1832.6 1.5 copy.98
  1835.3 1.5 copy.99
  (186 shorter events, 28.2 us)
Async XLA Ops:
  7.2 51.0 %copy-start = (bf16[1152,864]{0,1:T(8,128)(2,1)S(1)}, bf16[1152,864]{0,1:T(8,128)(2,1)}, u32[]{:S(2)}) copy-start(bf16[1152,864]{0,1:T(8,128)(2,1)} %param.17) | copy-start | bytes 5971972
  7.2 4.7 copy-start.40
  7.2 4.1 copy-start.36
  7.2 7.9 copy-start.44
  7.2 8.2 copy-start.45
  7.2 8.4 copy-start.43
  7.2 8.7 copy-start.41
  7.3 49.6 %copy-start.2 = (bf16[1,2,256,1152]{3,2,1,0:T(8,128)(2,1)S(1)}, bf16[1,2,256,1152]{3,2,1,0:T(8,128)(2,1)}, u32[]{:S(2)}) copy-start(bf16[1,2,256,1152]{3,2,1,0:T(8,128)(2,1)} %param.14) | copy-start | bytes 3538948
  7.3 126.8 %all-gather.5.cloned.1.call-start = ((), (), s32[]{:S(2)}) async-start(), calls=%async_computation.4 | async-start | bytes 8957952 | tf_op jit(solution)/shard_map/all_gather | solution.py:140
  8.0 191.1 %all-gather.7.cloned.1.call-start = ((), (), s32[]{:S(2)}) async-start(), calls=%async_computation.5 | async-start | bytes 2985984 | tf_op jit(solution)/shard_map/all_gather | solution.py:141
  8.8 334.0 %all-gather.9.cloned.1.call-start = ((), (), s32[]{:S(2)}) async-start(), calls=%async_computation.6 | async-start | bytes 11943936 | tf_op jit(solution)/shard_map/all_gather | solution.py:142
  9.5 486.0 %all-gather.11.cloned.1.call-start = ((), (), s32[]{:S(2)}) async-start(), calls=%async_computation.7 | async-start | bytes 11943936 | tf_op jit(solution)/shard_map/all_gather | solution.py:143
  10.1 48.7 %copy-start.42 = (bf16[864]{0:T(1024)(128)(2,1)S(1)}, bf16[864]{0:T(1024)(128)(2,1)}, u32[]{:S(2)}) copy-start(bf16[864]{0:T(1024)(128)(2,1)} %param.18) | copy-start | bytes 5188
  10.1 666.0 %reduce-scatter.7.cloned.1.call-start = ((), (), s32[]{:S(2)}) async-start(), calls=%async_computation.9 | async-start | bytes 5971968 | tf_op jit(solution)/shard_map/reduce_scatter | solution.py:232
  11.3 82.2 %copy-start.27 = (f32[1152]{0:T(1024)}, f32[1152]{0:T(1024)S(1)}, u32[]{:S(2)}) copy-start(f32[1152]{0:T(1024)S(1)} %reduce.4) | copy-start | bytes 13828
  58.1 39.6 %copy-start.30 = (f32[512]{0:T(512)}, f32[512]{0:T(512)S(1)}, u32[]{:S(2)}) copy-start(f32[512]{0:T(512)S(1)} %rsqrt.27) | copy-start | bytes 6148
  58.1 39.6 %copy-start.32 = (f32[1,2,2,128]{3,1,2,0:T(2,128)}, f32[1,2,2,128]{3,1,2,0:T(2,128)S(1)}, u32[]{:S(2)}) copy-start(f32[1,2,2,128]{3,1,2,0:T(2,128)S(1)} %copy.73) | copy-start | bytes 6148
  93.5 4.2 copy-start.25
  179.3 3.3 copy-start.1
  179.3 3.3 copy-start.14
  495.5 18.9 %copy-start.4 = (f32[512,1152]{1,0:T(8,128)S(1)}, f32[512,1152]{1,0:T(8,128)}, u32[]{:S(2)}) copy-start(f32[512,1152]{1,0:T(8,128)} %copy-done.3) | copy-start | bytes 7077892
  526.7 1.4 copy-start.12
  527.2 1.9 copy-start.15
  533.2 375.4 %reduce-scatter.5.cloned.1.call-start = ((), (), s32[]{:S(2)}) async-start(), calls=%async_computation.8 | async-start | bytes 17915904 | tf_op jit(solution)/shard_map/reduce_scatter | solution.py:231
  533.6 1.6 copy-start.23
  549.7 13.8 slice-start
  556.4 4.9 copy-start.8
  556.4 7.1 slice-start.1
  570.4 2.5 copy-start.21
  571.1 1.8 copy-start.16
  580.9 678.4 %reduce-scatter.9.cloned.1.call-start = ((), (), s32[]{:S(2)}) async-start(), calls=%async_computation.10 | async-start | bytes 23887872 | tf_op jit(solution)/shard_map/reduce_scatter | solution.py:233
  594.0 1015.7 %reduce-scatter.11.cloned.1.call-start = ((), (), s32[]{:S(2)}) async-start(), calls=%async_computation.11 | async-start | bytes 23887872 | tf_op jit(solution)/shard_map/reduce_scatter | solution.py:234
  608.9 1216.4 %all-reduce.16.cloned.1.call-start = ((), (), s32[]{:S(2)}) async-start(), calls=%async_computation.12 | async-start | bytes 23887872 | tf_op jit(solution)/shard_map/psum | solution.py:247
  610.2 10.0 copy-start.35
  610.2 10.0 copy-start.31
  610.2 11.2 copy-start.13
  610.2 11.2 copy-start.19
  620.2 1.7 copy-start.5
  620.2 2.0 copy-start.10
  620.2 2.0 copy-start.26
  622.2 51.6 %copy-start.29 = (f32[1152]{0:T(1024)S(1)}, f32[1152]{0:T(1024)}, u32[]{:S(2)}) copy-start(f32[1152]{0:T(1024)} %get-tuple-element.94) | copy-start | bytes 13828
  1609.6 2.1 copy-start.11
  1609.6 2.1 copy-start.39
  1609.7 39.3 %copy-start.28 = (f32[1152]{0:T(1024)S(1)}, f32[1152]{0:T(1024)}, u32[]{:S(2)}) copy-start(f32[1152]{0:T(1024)} %copy-done.27) | copy-start | bytes 13828
  1825.2 4.5 copy-start.20
  1829.7 1.5 copy-start.24
  1829.7 2.9 copy-start.18
  1832.6 2.7 copy-start.17
  (9 other events, 9.5 us)
Sparse Core Ops, SparseCore 0:
  10.3 123.7 all-gather.4
  136.2 53.2 all-gather.6
  191.7 151.0 all-gather.8
  344.8 150.6 all-gather.10
  533.3 102.3 reduce-scatter.6
  639.9 268.5 reduce-scatter.4
  912.9 346.3 reduce-scatter.8
  1263.2 346.4 reduce-scatter.10
  1613.5 211.7 all-reduce.15
where the time goes:
time: 1850 us; the launch traced here: 1840 us
  waiting for transfers between devices  1410 us (76%)
  blocking collectives  159 us (9%)
  matrix products  158 us (9%)
  local copies, waits for them, and re-layouts  72.8 us (4%)
  between operations  20.8 us (1%)
  other arithmetic  20.4 us (1%)
    reduce_scatter x1, waiting for transfers between devices, on_device(): lax.psum_scatter(grad_fc1, 'fsdp', scatter_dimension=0, tiled=True)  351 us
    reduce_scatter x1, waiting for transfers between devices, on_device(): lax.psum_scatter(grad_fc2, 'fsdp', scatter_dimension=0, tiled=True)  350 us
    reduce_scatter x1, waiting for transfers between devices, on_device(): lax.psum_scatter(grad_wqkv, 'fsdp', scatter_dimension=0, tiled=True)  233 us
    psum x1, waiting for transfers between devices, on_device(): lax.psum((shards[0], shards[1], shards[2], shards[3], shards[4], shards[5...  163 us
    all_gather x1, waiting for transfers between devices, on_device(): lax.all_gather(w_fc2, 'fsdp', axis=0, tiled=True)  140 us
    all_gather x1, waiting for transfers between devices, on_device(): lax.all_gather(w_fc1, 'fsdp', axis=0, tiled=True)  136 us
    unnamed x3, blocking collectives  111 us
    unnamed x128, local copies, waits for them, and re-layouts  37.7 us
  transfers between devices with their start and end apart: 9, of which 7 were waited for; matrix products, arithmetic and copies ran while one was open for 11% of the time, Pallas kernels for 0%

commit v1 on v0

--- a/solution.py
+++ b/solution.py
@@ -4,6 +4,19 @@
 from jax.sharding import PartitionSpec as P
 
 HEAD_DIM = 72
+
+
+def collect(x, axis, dim):
+    ways = lax.axis_size(axis)
+    up = [(d, (d + 1) % ways) for d in range(ways)]
+    down = [(d, (d - 1) % ways) for d in range(ways)]
+    earlier, later = ([x], [x])
+    for _ in range(ways // 2):
+        earlier.append(lax.ppermute(earlier[-1], axis, up))
+    for _ in range((ways - 1) // 2):
+        later.append(lax.ppermute(later[-1], axis, down))
+    line = jnp.concatenate([*earlier[::-1], *later[1:]], axis=dim)
+    return jnp.roll(line, (lax.axis_index(axis) - ways // 2) * x.shape[dim], axis=dim)
 
 
 def layer_norm(field):
@@ -140,7 +153,7 @@
         lax.all_gather(w_qkv, "fsdp", axis=0, tiled=True),
         lax.all_gather(w_proj, "fsdp", axis=0, tiled=True),
         lax.all_gather(w_fc1, "fsdp", axis=0, tiled=True),
-        lax.all_gather(w_fc2, "fsdp", axis=0, tiled=True),
+        collect(w_fc2, "fsdp", 0),
         lax.all_gather(b_qv, "fsdp", axis=0, tiled=True),
         lax.all_gather(b_proj, "fsdp", axis=0, tiled=True),
         lax.all_gather(b_fc1, "fsdp", axis=0, tiled=True),

time: 1850 us -> 1960 us (1.059)
  waiting for transfers between devices: 1410 us -> 1480 us
  local copies, waits for them, and re-layouts: 72.8 us -> 109 us
    ppermute x0 -> x7, waiting for transfers between devices: none -> 251 us  [the longest x4 247 us: collect(): earlier.append(lax.ppermute(earlier[-1], axis, up))]
    reduce_scatter x1, waiting for transfers between devices: 233 us -> 68.3 us  [on_device(): lax.psum_scatter(grad_wqkv, 'fsdp', scatter_dimension=0, tiled=True)]
    psum x1, waiting for transfers between devices: 163 us -> 128 us  [on_device(): lax.psum((shards[0], shards[1], shards[2], shards[3], shards[4], shards[5...]
    unnamed x128 -> x165, local copies, waits for them, and re-layouts: 37.7 us -> 70.9 us
  transfers between devices with their start and end apart: 9 -> 16, of which waited for: 7 -> 13; matrix products, arithmetic and copies ran while one was open for 11% -> 12% of each run, Pallas kernels for 0% -> 0%
where the time goes in v1:
time: 1960 us; the launch traced here: 1950 us
  waiting for transfers between devices  1480 us (76%)
  blocking collectives  158 us (8%)
  matrix products  151 us (8%)
  local copies, waits for them, and re-layouts  109 us (6%)
  other arithmetic  25.5 us (1%)
  between operations  20.7 us (1%)
    reduce_scatter x1, waiting for transfers between devices, on_device(): lax.psum_scatter(grad_fc1, 'fsdp', scatter_dimension=0, tiled=True)  351 us
    reduce_scatter x1, waiting for transfers between devices, on_device(): lax.psum_scatter(grad_fc2, 'fsdp', scatter_dimension=0, tiled=True)  350 us
    ppermute x4, waiting for transfers between devices, collect(): earlier.append(lax.ppermute(earlier[-1], axis, up))  247 us
    all_gather x1, waiting for transfers between devices, on_device(): lax.all_gather(w_fc1, 'fsdp', axis=0, tiled=True)  146 us
    all_gather x1, waiting for transfers between devices, on_device(): lax.all_gather(w_fc2, 'fsdp', axis=0, tiled=True)  138 us
    psum x1, waiting for transfers between devices, on_device(): lax.psum((shards[0], shards[1], shards[2], shards[3], shards[4], shards[5...  128 us
    unnamed x3, blocking collectives  111 us
    unnamed x165, local copies, waits for them, and re-layouts  70.9 us
  transfers between devices with their start and end apart: 16, of which 13 were waited for; matrix products, arithmetic and copies ran while one was open for 12% of the time, Pallas kernels for 0%

profile of v1, /device:TPU:0, one launch (start us, length us, event | category | flops | bytes accessed | tf_op | source)
XLA Modules:
  0.0 1952.2 jit_solution(4138245054828328226)
XLA Ops:
  15.8 40.8 %all-reduce.13 = (bf16[2304]{0:T(1024)(128)(2,1)S(1)}, bf16[1152]{0:T(1024)(128)(2,1)S(1)}, bf16[4608]{0:T(1024)(128)(2,1)S(1)}, bf16[1152]{0:T(1024)(128)(2,1)}) all-reduce(bf16[2304]{0:T(1024)(128)(2,1)S(1)} %dynamic-update-slice.1, bf16[1152]{0:T(1024)(128)(2,1)S(1)} %dynamic-update-slice.2, ...), channel_id=1, replica_groups=mesh['bin'=4,'fsdp'=8] {'fsdp'}, use_global_device_ids=true, to_apply=%add.1 | all-reduce | flops 9216 | bytes 36864
  58.1 34.3 %all-reduce = f32[6912]{0:T(1024)S(1)} all-reduce(f32[6912]{0:T(1024)S(1)} %add_dynamic-update-slice_fusion), channel_id=1, replica_groups=mesh['bin'=4,'fsdp'=8] {'fsdp'}, use_global_device_ids=true, to_apply=%add | all-reduce | flops 6912 | bytes 55296
  95.6 38.4 %all-gather.5.cloned.1.call-done = bf16[1152,3456]{1,0:T(8,128)(2,1)} async-done(((bf16[144,3456]{1,0:T(8,128)(2,1)}), bf16[1152,3456]{1,0:T(8,128)(2,1)}) %all-gather.5.cloned.1.call-update) | async-done | bytes 7962640 | tf_op jit(solution)/shard_map/all_gather | solution.py:153
  134.0 10.3 add_convert_fusion
  144.3 13.6 reshape.274
  157.9 6.0 fusion.77
  163.9 4.1 copy.71
  168.0 4.1 copy.72
  172.1 4.1 copy.70
  176.3 2.9 multiply_reduce_fusion.1
  189.5 5.6 fusion.76
  196.9 145.9 %all-gather.9.cloned.1.call-done = bf16[1152,4608]{1,0:T(8,128)(2,1)} async-done(((bf16[144,4608]{1,0:T(8,128)(2,1)}), bf16[1152,4608]{1,0:T(8,128)(2,1)}) %all-gather.9.cloned.1.call-update) | async-done | bytes 10616848 | tf_op jit(solution)/shard_map/all_gather | solution.py:155
  342.8 14.4 multiply_convert_fusion
  357.2 138.3 %all-gather.11.cloned.1.call-done = bf16[4608,1152]{1,0:T(8,128)(2,1)} async-done(((bf16[576,1152]{1,0:T(8,128)(2,1)}), bf16[4608,1152]{1,0:T(8,128)(2,1)}) %all-gather.11.cloned.1.call-update) | async-done | bytes 10616848 | tf_op jit(solution)/shard_map/all_gather | solution.py:171
  495.5 18.2 convert_reduce_fusion
  513.7 12.3 multiply_reduce_fusion.2
  530.6 4.0 fusion.83
  536.3 4.7 convolution_convert_fusion
  541.0 5.8 reshape.275
  546.9 4.1 copy.56
  551.0 6.7 multiply_reduce_fusion
  557.7 4.8 multiply_convert_fusion.1
  568.1 3.6 copy.61
  574.3 8.0 fusion.82
  582.4 13.0 fusion.72
  595.4 13.3 fusion.60
  609.4 54.5 %collective-permute-done = bf16[576,1152]{1,0:T(8,128)(2,1)S(1)} collective-permute-done((bf16[576,1152]{1,0:T(8,128)(2,1)}, bf16[576,1152]{1,0:T(8,128)(2,1)S(1)}, u32[]{:S(2)}, u32[]{:S(2)}) %collective-permute-start) | collective-permute-done | bytes 1327136 | tf_op jit(solution)/shard_map/ppermute | solution.py:15
  665.0 4.7 collective-permute-start.4
  669.7 63.7 %collective-permute-done.1 = bf16[576,1152]{1,0:T(8,128)(2,1)S(1)} collective-permute-done((bf16[576,1152]{1,0:T(8,128)(2,1)S(1)}, bf16[576,1152]{1,0:T(8,128)(2,1)S(1)}, u32[]{:S(2)}, u32[]{:S(2)}) %collective-permute-start.1) | collective-permute-done | bytes 1327136 | tf_op jit(solution)/shard_map/ppermute | solution.py:15
  737.0 3.9 collective-permute-done.4
  740.9 68.2 %collective-permute-done.2 = bf16[576,1152]{1,0:T(8,128)(2,1)} collective-permute-done((bf16[576,1152]{1,0:T(8,128)(2,1)S(1)}, bf16[576,1152]{1,0:T(8,128)(2,1)}, u32[]{:S(2)}, u32[]{:S(2)}) %collective-permute-start.2) | collective-permute-done | bytes 1327136 | tf_op jit(solution)/shard_map/ppermute | solution.py:15
  809.1 2.6 collective-permute-start.3
  818.2 60.9 %collective-permute-done.3 = bf16[576,1152]{1,0:T(8,128)(2,1)} collective-permute-done((bf16[576,1152]{1,0:T(8,128)(2,1)}, bf16[576,1152]{1,0:T(8,128)(2,1)}, u32[]{:S(2)}, u32[]{:S(2)}) %collective-permute-start.3) | collective-permute-done | bytes 1327136 | tf_op jit(solution)/shard_map/ppermute | solution.py:15
  887.7 3.0 constant_dynamic-update-slice_fusion.10
  890.8 9.1 fusion.45
  902.5 8.5 fusion.50
  911.0 35.5 %all-reduce.5 = f32[6912]{0:T(1024)S(1)} all-reduce(f32[6912]{0:T(1024)S(1)} %constant_dynamic-update-slice_fusion.17), channel_id=2, replica_groups=mesh['bin'=4,'fsdp'=8] {'fsdp'}, use_global_device_ids=true, to_apply=%region_17.18.clone | all-reduce | flops 6912 | bytes 55296
  949.0 68.3 %reduce-scatter.5.cloned.1.call-done = f32[144,3456]{1,0:T(8,128)} async-done(((f32[1152,3456]{1,0:T(8,128)}), f32[144,3456]{1,0:T(8,128)}) %reduce-scatter.5.cloned.1.call-update) | async-done | bytes 1990672 | tf_op jit(solution)/shard_map/reduce_scatter | solution.py:244
  1017.3 350.7 %reduce-scatter.9.cloned.1.call-done = f32[144,4608]{1,0:T(8,128)} async-done(((f32[1152,4608]{1,0:T(8,128)}), f32[144,4608]{1,0:T(8,128)}) %reduce-scatter.9.cloned.1.call-update) | async-done | bytes 2654224 | tf_op jit(solution)/shard_map/reduce_scatter | solution.py:246
  1368.0 350.3 %reduce-scatter.11.cloned.1.call-done = f32[576,1152]{1,0:T(8,128)} async-done(((f32[4608,1152]{1,0:T(8,128)}), f32[576,1152]{1,0:T(8,128)}) %reduce-scatter.11.cloned.1.call-update) | async-done | bytes 2654224 | tf_op jit(solution)/shard_map/reduce_scatter | solution.py:247
  1723.2 2.6 constant_dynamic-update-slice_fusion.7
  1725.9 3.0 constant_dynamic-update-slice_fusion.6
  1741.1 35.3 %all-reduce.10 = (f32[1152]{0:T(1024)S(1)}, f32[2304]{0:T(1024)S(1)}, f32[1152]{0:T(1024)S(1)}, f32[4608]{0:T(1024)S(1)}, f32[1152]{0:T(1024)S(1)}) all-reduce(f32[1152]{0:T(1024)S(1)} %convolution_reduce_fusion, f32[2304]{0:T(1024)S(1)} %pad_maximum_fusion, ...), channel_id=1, replica_groups=mesh['bin'=4,'fsdp'=8] {'fsdp'}, use_global_device_ids=true, to_apply=%region_18.19 | all-reduce | flops 10368 | bytes 82944 | tf_op jit(solution)/shard_map/psum | solution.py:257
  1777.4 11.7 all-reduce.11
  1789.1 4.5 add_add_fusion.2
  1793.6 12.4 fusion.28
  1806.0 127.9 %all-reduce.16.cloned.1.call-done = (f32[1152,864]{0,1:T(8,128)}, f32[144,3456]{1,0:T(8,128)}, f32[144,1152]{1,0:T(8,128)}, f32[144,4608]{1,0:T(8,128)}, f32[576,1152]{1,0:T(8,128)}) async-done(((f32[1152,864]{0,1:T(8,128)}, f32[144,3456]{1,0:T(8,128)}, f32[144,1152]{1,0:T(8,128)}, f32[144,4608]{1,0:T(8,128)}, f32[576,1152]{1,0:T(8,128)}), (f32[1152,864]{0,1:T(8,128)}, f32[144,3456]{1,0:T(8,128)}, ...) | async-done | bytes 11943952 | tf_op jit(solution)/shard_map/psum | solution.py:260
  1933.9 4.5 copy.110
  (241 shorter events, 84.3 us)
Async XLA Ops:
  7.2 50.2 %copy-start = (bf16[1152,864]{0,1:T(8,128)(2,1)S(1)}, bf16[1152,864]{0,1:T(8,128)(2,1)}, u32[]{:S(2)}) copy-start(bf16[1152,864]{0,1:T(8,128)(2,1)} %param.17) | copy-start | bytes 5971972
  7.2 6.1 copy-start.43
  7.2 6.8 copy-start.2
  7.2 126.7 %all-gather.5.cloned.1.call-start = ((), (), s32[]{:S(2)}) async-start(), calls=%async_computation.4 | async-start | bytes 8957952 | tf_op jit(solution)/shard_map/all_gather | solution.py:153
  8.0 181.5 %all-gather.7.cloned.1.call-start = ((), (), s32[]{:S(2)}) async-start(), calls=%async_computation.5 | async-start | bytes 2985984 | tf_op jit(solution)/shard_map/all_gather | solution.py:154
  8.7 6.1 copy-start.51
  8.7 6.3 copy-start.52
  8.7 6.6 copy-start.48
  8.7 6.8 copy-start.50
  8.8 334.0 %all-gather.9.cloned.1.call-start = ((), (), s32[]{:S(2)}) async-start(), calls=%async_computation.6 | async-start | bytes 11943936 | tf_op jit(solution)/shard_map/all_gather | solution.py:155
  9.5 486.0 %all-gather.11.cloned.1.call-start = ((), (), s32[]{:S(2)}) async-start(), calls=%async_computation.7 | async-start | bytes 11943936 | tf_op jit(solution)/shard_map/all_gather | solution.py:171
  10.1 47.9 %copy-start.49 = (bf16[864]{0:T(1024)(128)(2,1)S(1)}, bf16[864]{0:T(1024)(128)(2,1)}, u32[]{:S(2)}) copy-start(bf16[864]{0:T(1024)(128)(2,1)} %param.18) | copy-start | bytes 5188
  10.1 938.9 %reduce-scatter.7.cloned.1.call-start = ((), (), s32[]{:S(2)}) async-start(), calls=%async_computation.9 | async-start | bytes 5971968 | tf_op jit(solution)/shard_map/reduce_scatter | solution.py:245
  13.4 79.1 %copy-start.34 = (f32[1152]{0:T(1024)}, f32[1152]{0:T(1024)S(1)}, u32[]{:S(2)}) copy-start(f32[1152]{0:T(1024)S(1)} %reduce.4) | copy-start | bytes 13828
  14.7 79.2 %copy-start.36 = (f32[512]{0:T(512)}, f32[512]{0:T(512)S(1)}, u32[]{:S(2)}) copy-start(f32[512]{0:T(512)S(1)} %rsqrt.27) | copy-start | bytes 6148
  14.8 79.2 %copy-start.38 = (f32[1,2,2,128]{3,1,2,0:T(2,128)}, f32[1,2,2,128]{3,1,2,0:T(2,128)S(1)}, u32[]{:S(2)}) copy-start(f32[1,2,2,128]{3,1,2,0:T(2,128)S(1)} %copy.73) | copy-start | bytes 6148
  57.2 38.4 %copy-start.45 = (f32[2]{0:T(128)}, f32[2]{0:T(128)S(1)}, u32[]{:S(2)}) copy-start(f32[2]{0:T(128)S(1)} %compare_convert_fusion) | copy-start | bytes 28
  495.5 18.2 copy-start.4
  513.7 12.3 copy-start.53
  534.7 482.6 %reduce-scatter.5.cloned.1.call-start = ((), (), s32[]{:S(2)}) async-start(), calls=%async_computation.8 | async-start | bytes 17915904 | tf_op jit(solution)/shard_map/reduce_scatter | solution.py:244
  551.0 14.2 slice-start
  557.7 4.9 copy-start.13
  557.7 7.6 slice-start.1
  582.3 785.7 %reduce-scatter.9.cloned.1.call-start = ((), (), s32[]{:S(2)}) async-start(), calls=%async_computation.10 | async-start | bytes 23887872 | tf_op jit(solution)/shard_map/reduce_scatter | solution.py:246
  595.4 1122.9 %reduce-scatter.11.cloned.1.call-start = ((), (), s32[]{:S(2)}) async-start(), calls=%async_computation.11 | async-start | bytes 23887872 | tf_op jit(solution)/shard_map/reduce_scatter | solution.py:247
  608.7 202.9 %copy-start.44 = (bf16[1152]{0:T(1024)(128)(2,1)S(1)}, bf16[1152]{0:T(1024)(128)(2,1)}, u32[]{:S(2)}) copy-start(bf16[1152]{0:T(1024)(128)(2,1)} %get-tuple-element.91) | copy-start | bytes 6916
  608.7 205.5 %copy-start.46 = (f32[2]{0:T(128)S(1)}, f32[2]{0:T(128)}, u32[]{:S(2)}) copy-start(f32[2]{0:T(128)} %copy-done.45) | copy-start | bytes 28
  608.8 1325.1 %all-reduce.16.cloned.1.call-start = ((), (), s32[]{:S(2)}) async-start(), calls=%async_computation.12 | async-start | bytes 23887872 | tf_op jit(solution)/shard_map/psum | solution.py:260
  608.8 55.1 %collective-permute-start = (bf16[576,1152]{1,0:T(8,128)(2,1)}, bf16[576,1152]{1,0:T(8,128)(2,1)S(1)}, u32[]{:S(2)}, u32[]{:S(2)}) collective-permute-start(bf16[576,1152]{1,0:T(8,128)(2,1)} %param.25), channel_id=1, source_target_pairs={{0,1},{1,2},{2,3},{3,4},{4,5},{5,6},{6,7},{7,0},{8,9},{9,10},{10,1... | collective-permute-start | bytes 3981320 | tf_op jit(solution)/shard_map/ppermute | solution.py:15
  665.0 68.5 %collective-permute-start.1 = (bf16[576,1152]{1,0:T(8,128)(2,1)S(1)}, bf16[576,1152]{1,0:T(8,128)(2,1)S(1)}, u32[]{:S(2)}, u32[]{:S(2)}) collective-permute-start(bf16[576,1152]{1,0:T(8,128)(2,1)S(1)} %collective-permute-done), channel_id=1, source_target_pairs={{0,1},{1,2},{2,3},{3,4},{4,5},{5,6},{6,7},{7,0},{8,9},{9,10},{10,1... | collective-permute-start | bytes 3981320 | tf_op jit(solution)/shard_map/ppermute | solution.py:15
  665.0 75.9 %collective-permute-start.4 = (bf16[576,1152]{1,0:T(8,128)(2,1)}, bf16[576,1152]{1,0:T(8,128)(2,1)}, u32[]{:S(2)}, u32[]{:S(2)}) collective-permute-start(bf16[576,1152]{1,0:T(8,128)(2,1)} %param.25), channel_id=1, source_target_pairs={{0,7},{1,0},{2,1},{3,2},{4,3},{5,4},{6,5},{7,6},{8,15},{9,8},{10,9... | collective-permute-start | bytes 3981320 | tf_op jit(solution)/shard_map/ppermute | solution.py:17
  734.5 74.6 %collective-permute-start.2 = (bf16[576,1152]{1,0:T(8,128)(2,1)S(1)}, bf16[576,1152]{1,0:T(8,128)(2,1)}, u32[]{:S(2)}, u32[]{:S(2)}) collective-permute-start(bf16[576,1152]{1,0:T(8,128)(2,1)S(1)} %collective-permute-done.1), channel_id=1, source_target_pairs={{0,1},{1,2},{2,3},{3,4},{4,5},{5,6},{6,7},{7,0},{8,9},{9,10},{10,1... | collective-permute-start | bytes 3981320 | tf_op jit(solution)/shard_map/ppermute | solution.py:15
  740.9 75.1 %collective-permute-start.5 = (bf16[576,1152]{1,0:T(8,128)(2,1)}, bf16[576,1152]{1,0:T(8,128)(2,1)}, u32[]{:S(2)}, u32[]{:S(2)}) collective-permute-start(bf16[576,1152]{1,0:T(8,128)(2,1)} %collective-permute-done.4), channel_id=1, source_target_pairs={{0,7},{1,0},{2,1},{3,2},{4,3},{5,4},{6,5},{7,6},{8,15},{9,8},{10,9... | collective-permute-start | bytes 3981320 | tf_op jit(solution)/shard_map/ppermute | solution.py:17
  809.1 70.0 %collective-permute-start.3 = (bf16[576,1152]{1,0:T(8,128)(2,1)}, bf16[576,1152]{1,0:T(8,128)(2,1)}, u32[]{:S(2)}, u32[]{:S(2)}) collective-permute-start(bf16[576,1152]{1,0:T(8,128)(2,1)} %collective-permute-done.2), channel_id=1, source_target_pairs={{0,1},{1,2},{2,3},{3,4},{4,5},{5,6},{6,7},{7,0},{8,9},{9,10},{10,1... | collective-permute-start | bytes 3981320 | tf_op jit(solution)/shard_map/ppermute | solution.py:15
  816.0 68.2 %copy-start.20 = (bf16[576,1152]{1,0:T(8,128)(2,1)S(1)}, bf16[576,1152]{1,0:T(8,128)(2,1)}, u32[]{:S(2)}) copy-start(bf16[576,1152]{1,0:T(8,128)(2,1)} %copy-done.19) | copy-start | bytes 3981316
  816.0 904.8 %collective-permute-start.6 = (bf16[576,1152]{1,0:T(8,128)(2,1)}, bf16[576,1152]{1,0:T(8,128)(2,1)}, u32[]{:S(2)}, u32[]{:S(2)}) collective-permute-start(bf16[576,1152]{1,0:T(8,128)(2,1)} %collective-permute-done.5), channel_id=1, source_target_pairs={{0,7},{1,0},{2,1},{3,2},{4,3},{5,4},{6,5},{7,6},{8,15},{9,8},{10,9... | collective-permute-start | bytes 3981320 | tf_op jit(solution)/shard_map/ppermute | solution.py:17
  886.6 4.2 copy-start.39
  887.7 13.4 slice-start.2
  890.8 9.2 copy-start.42
  890.8 9.2 copy-start.37
  890.8 10.4 slice-start.3
  890.8 10.4 slice-start.4
  899.9 11.1 copy-start.14
  902.5 44.1 %copy-start.40 = (f32[1152]{0:T(1024)S(1)}, f32[1152]{0:T(1024)}, u32[]{:S(2)}) copy-start(f32[1152]{0:T(1024)} %get-tuple-element.92) | copy-start | bytes 13828
  1723.2 5.7 copy-start.21
  1737.5 39.1 %copy-start.35 = (f32[1152]{0:T(1024)S(1)}, f32[1152]{0:T(1024)}, u32[]{:S(2)}) copy-start(f32[1152]{0:T(1024)} %copy-done.34) | copy-start | bytes 13828
  1789.1 4.5 copy-start.5
  1933.9 4.5 copy-start.29
  (27 other events, 60.2 us)
Sparse Core Ops, SparseCore 0:
  10.2 123.6 all-gather.4
  136.1 53.3 all-gather.6
  191.7 151.0 all-gather.8
  344.8 150.6 all-gather.10
  534.8 107.5 reduce-scatter.6
  646.6 370.5 reduce-scatter.4
  1021.6 346.2 reduce-scatter.8
  1371.9 346.3 reduce-scatter.10
  1722.1 211.7 all-reduce.15
